TPU v7x, 32 devices: a whole 2x2x4 slice. The times are simulated.
32 devices in a mesh: gx: 8 (over z, y), gy: 2 (over x), gz: 2 (over core).
Axes of the slice: x: 2, y: 2, z: 4, core: 2. Of those that a mesh axis runs over, the one named last changes fastest.
Arguments:
- tensor_blocks: bfloat16 [8, 2, 2, 2, 128, 128, 128], P('gx', 'gy', 'gz'), may hold values from -768 to 768
- block_coords: int32 [8, 2, 2, 2, 3], P('gx', 'gy', 'gz'), may hold values from 0 to 1, as said below
- live_counts: int32 [8, 2, 2], P('gx', 'gy', 'gz'), may hold values from 1 to 2, as said below
- factor_a: bfloat16 [8, 256, 256], P('gx', ('gy', 'gz')), may hold values from 0.049804688 to 1
- factor_b: bfloat16 [2, 256, 256], P('gy', ('gx', 'gz')), may hold values from 0.049804688 to 1
- factor_c: bfloat16 [2, 256, 256], P('gz', ('gx', 'gy')), may hold values from 0.049804688 to 1
Outputs:
- updated_a: bfloat16 [8, 256, 256], P('gx', ('gy', 'gz'))
- updated_b: bfloat16 [2, 256, 256], P('gy', ('gx', 'gz'))
- updated_c: bfloat16 [2, 256, 256], P('gz', ('gx', 'gy'))
Inputs may be any that keep to these rules, and one draw needn't show every extreme that they name: `block_coords`: within one cell the 2 slots hold distinct positions. `live_counts`: some cell has exactly 2 live slots and another exactly one.
All inputs are finite; a program needn't handle non-finite values. Where the computation divides by a largest or mean magnitude, that divisor is 1e-20 or more.
Results may differ from a plain program's by a relative error of at most 0.0055.
Values may be sent and summed in bfloat16 or wider, within the bound.
No kernel may reach another device: no remote copies, remote signals or barrier semaphores. Data moves between devices by JAX's collectives and lax.ppermute only.
A program may use at most 256 MiB of HBM per device.

v0:
```python
import jax
import jax.numpy as jnp
from jax import lax
from jax.sharding import PartitionSpec as P

NS_STEPS = 8
ADMM_ITERS = 4
HIGHEST = lax.Precision.HIGHEST


def gram_rows(factor):
    return lax.dot_general(
        factor, factor, (((0,), (0,)), ((), ())), preferred_element_type=jnp.float32
    )


def newton_inverse(gram_left, gram_right):
    weighted = gram_left * gram_right
    width = weighted.shape[0]
    identity = jnp.eye(width, dtype=weighted.dtype)
    penalty = jnp.trace(weighted) / width
    system = weighted + penalty * identity
    bound = jnp.max(jnp.sum(jnp.abs(system), axis=1))
    inverse = identity / bound
    for step in range(NS_STEPS):
        inverse = jnp.dot(
            inverse, 2.0 * identity - jnp.dot(system, inverse, precision=HIGHEST), precision=HIGHEST
        )
    return (penalty, inverse)


def split_updates(totals, start, penalty, inverse):
    primal = start.astype(jnp.float32)
    dual = jnp.zeros_like(primal)
    for step in range(ADMM_ITERS):
        target = jnp.dot(totals + penalty * (primal + dual), inverse, precision=HIGHEST)
        primal = jnp.maximum(target - dual, 0.0)
        dual = dual + primal - target
    return primal.astype(jnp.bfloat16)


def on_device(tensor_blocks, block_coords, live_counts, factor_a, factor_b, factor_c):
    slot_count = tensor_blocks.shape[3]
    side = tensor_blocks.shape[4]
    width = factor_a.shape[2]
    blocks = tensor_blocks.reshape(slot_count, side, side, side)
    triples = block_coords.reshape(slot_count, 3)
    live_total = live_counts.reshape(())
    own_a = factor_a[0]
    own_b = factor_b[0]
    own_c = factor_c[0]
    slab_b = lax.all_gather(own_b, ("gx", "gz"), axis=0, tiled=True)
    slab_c = lax.all_gather(own_c, ("gx", "gy"), axis=0, tiled=True)
    height = slab_b.shape[0]
    gram_b = lax.psum(gram_rows(slab_b), "gy")
    gram_c = lax.psum(gram_rows(slab_c), "gz")

    def fetch(position):
        block = lax.dynamic_index_in_dim(blocks, position, 0, keepdims=False)
        triple = lax.dynamic_index_in_dim(triples, position, 0, keepdims=False)
        return (block, triple * side)

    def accumulate(running, row_start, terms):
        current = lax.dynamic_slice_in_dim(running, row_start, side, 0)
        return lax.dynamic_update_slice_in_dim(running, current + terms, row_start, 0)

    def first_visit(position, running):
        block, starts = fetch(position)
        band_b = lax.dynamic_slice_in_dim(slab_b, starts[1], side, 0)
        band_c = lax.dynamic_slice_in_dim(slab_c, starts[2], side, 0)
        contracted = jnp.dot(
            block.reshape(side * side, side), band_c, preferred_element_type=jnp.float32
        ).reshape(side, side, width)
        terms = jnp.sum(contracted * band_b.astype(jnp.float32)[None], axis=1)
        return accumulate(running, starts[0], terms)

    empty = jnp.zeros((height, width), jnp.float32)
    partial_a = lax.fori_loop(0, live_total, first_visit, empty)
    sums_a = lax.psum_scatter(partial_a, ("gy", "gz"), scatter_dimension=0, tiled=True)
    penalty, inverse = newton_inverse(gram_b, gram_c)
    new_a = split_updates(sums_a, own_a, penalty, inverse)
    slab_a = lax.all_gather(new_a, ("gy", "gz"), axis=0, tiled=True)
    gram_a = lax.psum(gram_rows(slab_a), "gx")

    def second_visit(position, state):
        running, stored = state
        block, starts = fetch(position)
        band_a = lax.dynamic_slice_in_dim(slab_a, starts[0], side, 0)
        band_c = lax.dynamic_slice_in_dim(slab_c, starts[2], side, 0)
        projected = lax.dot_general(
            band_a,
            block.reshape(side, side * side),
            (((0,), (0,)), ((), ())),
            preferred_element_type=jnp.float32,
        )
        terms = jnp.sum(
            projected.reshape(width, side, side) * band_c.astype(jnp.float32).T[:, None, :], axis=2
        ).T
        stored = lax.dynamic_update_index_in_dim(stored, projected, position, 0)
        return (accumulate(running, starts[1], terms), stored)

    holder = jnp.zeros((slot_count, width, side * side), jnp.float32)
    partial_b, stored = lax.fori_loop(0, live_total, second_visit, (empty, holder))
    sums_b = lax.psum_scatter(partial_b, ("gx", "gz"), scatter_dimension=0, tiled=True)
    penalty, inverse = newton_inverse(gram_a, gram_c)
    new_b = split_updates(sums_b, own_b, penalty, inverse)
    slab_b_new = lax.all_gather(new_b, ("gx", "gz"), axis=0, tiled=True)
    gram_b_new = lax.psum(gram_rows(slab_b_new), "gy")

    def third_visit(position, running):
        projected = lax.dynamic_index_in_dim(stored, position, 0, keepdims=False)
        starts = lax.dynamic_index_in_dim(triples, position, 0, keepdims=False) * side
        band_b = lax.dynamic_slice_in_dim(slab_b_new, starts[1], side, 0)
        terms = jnp.sum(
            projected.reshape(width, side, side) * band_b.astype(jnp.float32).T[:, :, None], axis=1
        ).T
        return accumulate(running, starts[2], terms)

    partial_c = lax.fori_loop(0, live_total, third_visit, empty)
    sums_c = lax.psum_scatter(partial_c, ("gx", "gy"), scatter_dimension=0, tiled=True)
    penalty, inverse = newton_inverse(gram_a, gram_b_new)
    new_c = split_updates(sums_c, own_c, penalty, inverse)
    return (new_a[None], new_b[None], new_c[None])


def solution(mesh):
    return jax.shard_map(
        on_device,
        mesh=mesh,
        in_specs=(
            P("gx", "gy", "gz", None, None, None, None),
            P("gx", "gy", "gz", None, None),
            P("gx", "gy", "gz"),
            P("gx", ("gy", "gz"), None),
            P("gy", ("gx", "gz"), None),
            P("gz", ("gx", "gy"), None),
        ),
        out_specs=(
            P("gx", ("gy", "gz"), None),
            P("gy", ("gx", "gz"), None),
            P("gz", ("gx", "gy"), None),
        ),
        check_vma=False,
    )
```

profile of v0, /device:TPU:0, one launch (start us, length us, event | category | flops | bytes accessed | tf_op | source)
XLA Modules:
  0.0 451.7 jit_solution(6024621092706022354)
XLA Ops:
  8.0 43.3 %all-gather = bf16[1,256,256]{2,1,0:T(8,128)(2,1)S(1)} all-gather(bf16[1,16,256]{2,1,0:T(8,128)(2,1)} %param.17), channel_id=2, replica_groups=mesh['gx'=8,'gy'=2,'gz'=2] {'gx','gy'}, dimensions={1}, use_global_device_ids=true | all-gather | bytes 139264 | tf_op jit(solution)/shard_map/all_gather | solution.py:53
  52.4 17.8 %all-gather.1 = bf16[1,256,256]{2,1,0:T(8,128)(2,1)S(1)} all-gather(bf16[1,16,256]{2,1,0:T(8,128)(2,1)} %param.16), channel_id=3, replica_groups=mesh['gx'=8,'gy'=2,'gz'=2] {'gx','gz'}, dimensions={1}, use_global_device_ids=true | all-gather | bytes 139264 | tf_op jit(solution)/shard_map/all_gather | solution.py:52
  71.2 14.1 %while.32 = (s32[]{:T(128)}, f32[256,256]{1,0:T(8,128)S(1)}, s32[]{:T(128)}, s32[2,3]{1,0:T(2,128)}, bf16[2,128,128,128]{3,2,1,0:T(8,128)(2,1)}, /*index=5*/bf16...) while((s32[]{:T(128)}, f32[256,256]{1,0:T(8,128)S(1)}, ...), condition=%wide.region_2.3_spmd, body=%wide.region_0.2_spmd.sunk | while | flops 1082163200 | bytes 5374269 | solution.py:78
  77.1 4.5 %multiply_reduce_fusion.4 = f32[128,256]{1,0:T(8,128)S(1)} fusion(f32[128,256]{1,0:T(8,128)S(1)} %dynamic-slice_convert_fusion.2, bf16[2,128,128,128]{3,2,1,0:T(8,128)(2,1)} %get-tuple-element.385, s32[]{:T(128)S(6)} %select_n.72, bf16[256,256]{1,0:T(8,128)(2,1)S(1)} %get-tuple-element.386, s32[]{:T(128)S(6)} %select_n.74), kind=kOutput, calls=%fused_computation.clone.1 | convolution fusion | flops 1082097664 | bytes 4521992 | tf_op jit(solution)/shard_map/while/body/dot_general | solution.py:71
  86.1 7.3 %all-reduce.5.cloned.1.call-done = f32[256,256]{1,0:T(8,128)} async-done(((f32[256,256]{1,0:T(8,128)}), f32[256,256]{1,0:T(8,128)}) %all-reduce.5.cloned.1.call-update) | async-done | bytes 262160 | tf_op jit(solution)/shard_map/psum | solution.py:55
  93.4 1.7 select_reduce_fusion.2
  103.5 13.3 %reduce-scatter.4.cloned.1.call-done = f32[64,256]{1,0:T(8,128)} async-done(((f32[256,256]{1,0:T(8,128)}), f32[64,256]{1,0:T(8,128)}) %reduce-scatter.4.cloned.1.call-update) | async-done | bytes 65552 | tf_op jit(solution)/shard_map/reduce_scatter | solution.py:79
  121.2 5.4 %all_gather.14 = bf16[256,256]{1,0:T(8,128)(2,1)S(1)} all-gather(bf16[64,256]{1,0:T(8,128)(2,1)S(1)} %fusion.15), channel_id=1, replica_groups=mesh['gx'=8,'gy'=2,'gz'=2] {'gy','gz'}, dimensions={0}, use_global_device_ids=true | all-gather | bytes 163840 | tf_op jit(solution)/shard_map/all_gather | solution.py:82
  127.6 11.0 %broadcast_in_dim.28 = f32[2,256,16384]{2,1,0:T(8,128)} broadcast(f32[]{:T(128)} %constant.86.clone.1), dimensions={} | broadcast | bytes 33554436 | tf_op jit(solution)/shard_map/broadcast_in_dim | solution.py:102
  138.7 49.5 %while.33 = (s32[]{:T(128)}, f32[256,256]{1,0:T(8,128)S(1)}, f32[2,256,16384]{2,1,0:T(8,128)}, s32[]{:T(128)}, s32[2,3]{1,0:T(2,128)S(1)}, /*index=5*/bf16[256,2...) while((s32[]{:T(128)}, f32[256,256]{1,0:T(8,128)S(1)}, ...), condition=%wide.region_11.12_spmd, body=%wide.region_9.11_spmd.sunk | while | flops 1082163200 | bytes 98697544 | solution.py:103
  142.3 2.5 constant_dynamic-slice_fusion.14
  144.8 15.0 %bitcast_dynamic-update-slice_fusion.2 = (f32[2,256,16384]{2,1,0:T(8,128)}, f32[256,16384]{1,0:T(8,128)}) fusion(f32[2,256,16384]{2,1,0:T(8,128)} %get-tuple-element.406, s32[]{:T(128)S(6)} %select_n.76, bf16[16,8,128,128]{3,2,1,0:T(8,128)(2,1)S(1)} %bitcast.188, bf16[256,256]{1,0:T(8,128)(2,1)S(1)} %get-tuple-element.421, s32[]{:T(128)S(6)} %select_n.78), kind=kOutput, calls=%fused_computation.10.clone.1 | convolution fusion | flops 1073741824 | bytes 37814280 | tf_op jit(solution)/shard_map/while/body/dot_general | solution.py:90
  159.8 14.1 %copy.52 = f32[32,8,128,128]{3,2,1,0:T(8,128)} copy(f32[32,8,128,128]{3,1,2,0:T(8,128)} %bitcast.187) | data formatting | bytes 33554432 | tf_op jit(solution)/shard_map/while
  176.0 8.2 %multiply_reduce_fusion.5 = f32[256,128]{1,0:T(8,128)S(1)} fusion(f32[256,128,128]{2,1,0:T(8,128)} %bitcast.186, f32[256,128]{1,0:T(8,128)S(1)} %convert_bitcast_fusion.4), kind=kLoop, calls=%fused_computation.11.clone.1 | loop fusion | flops 8355840 | bytes 17039360 | tf_op jit(solution)/shard_map/while/body/reduce_sum | solution.py:96
  189.2 9.5 %all-reduce.9.cloned.1.call-done = f32[256,256]{1,0:T(8,128)} async-done(((f32[256,256]{1,0:T(8,128)}), f32[256,256]{1,0:T(8,128)}) %all-reduce.9.cloned.1.call-update) | async-done | bytes 262160 | tf_op jit(solution)/shard_map/psum | solution.py:83
  198.7 1.6 select_reduce_fusion.1
  208.7 84.3 %reduce-scatter.6.cloned.1.call-done = f32[16,256]{1,0:T(8,128)} async-done(((f32[256,256]{1,0:T(8,128)}), f32[16,256]{1,0:T(8,128)}) %reduce-scatter.6.cloned.1.call-update) | async-done | bytes 16400 | tf_op jit(solution)/shard_map/reduce_scatter | solution.py:104
  296.8 19.8 %all_gather.15 = bf16[256,256]{1,0:T(8,128)(2,1)S(1)} all-gather(bf16[16,256]{1,0:T(8,128)(2,1)S(1)} %fusion.18), channel_id=1, replica_groups=mesh['gx'=8,'gy'=2,'gz'=2] {'gx','gz'}, dimensions={0}, use_global_device_ids=true | all-gather | bytes 139264 | tf_op jit(solution)/shard_map/all_gather | solution.py:107
  317.6 24.1 %while.34 = (s32[]{:T(128)}, f32[256,256]{1,0:T(8,128)S(1)}, s32[]{:T(128)}, s32[2,3]{1,0:T(2,128)S(1)}, f32[2,256,16384]{2,1,0:T(8,128)}, /*index=5*/bf16[256,2...) while((s32[]{:T(128)}, f32[256,256]{1,0:T(8,128)S(1)}, s32[]{:T(128)}, ...), condition=%wide.region_19.20_spmd, body=%wide.region_17.19_spmd.sunk | while | flops 8421390 | bytes 86049016 | solution.py:119
  321.0 6.6 %dynamic-slice_bitcast_fusion.2 = f32[32,8,128,128]{3,1,2,0:T(8,128)S(1)} fusion(f32[2,256,16384]{2,1,0:T(8,128)} %get-tuple-element.452, s32[]{:T(128)S(6)} %select_n.80), kind=kLoop, calls=%fused_computation.26.clone.1 | loop fusion | bytes 33554436 | tf_op jit(solution)/shard_map/while
  327.7 3.8 copy.56
  331.5 6.1 %fusion.282 = f32[256,128]{1,0:T(8,128)S(1)} fusion(f32[32,8,128,128]{3,2,1,0:T(8,128)S(1)} %copy.56, f32[256,128]{1,0:T(8,128)S(1)} %convert_bitcast_fusion.5), kind=kLoop, calls=%fused_computation.25.clone.1 | loop fusion | flops 8355840 | bytes 17039360 | tf_op jit(solution)/shard_map/while/body/reduce_sum | solution.py:114
  342.4 1.6 select_reduce_fusion
  352.4 87.5 %reduce-scatter.8.cloned.1.call-done = f32[16,256]{1,0:T(8,128)} async-done(((f32[256,256]{1,0:T(8,128)}), f32[16,256]{1,0:T(8,128)}) %reduce-scatter.8.cloned.1.call-update) | async-done | bytes 16400 | tf_op jit(solution)/shard_map/reduce_scatter | solution.py:120
  (136 shorter events, 46.3 us)
Async XLA Ops:
  8.0 78.1 %all-reduce.7.cloned.1.call-start = ((), (), s32[]{:S(2)}) async-start(), calls=%async_computation.5 | async-start | bytes 524288 | tf_op jit(solution)/shard_map/psum | solution.py:56
  52.3 41.1 %all-reduce.5.cloned.1.call-start = ((), (), s32[]{:S(2)}) async-start(), calls=%async_computation.4 | async-start | bytes 524288 | tf_op jit(solution)/shard_map/psum | solution.py:55
  71.1 45.6 %reduce-scatter.4.cloned.1.call-start = ((), (), s32[]{:S(2)}) async-start(), calls=%async_computation.3 | async-start | bytes 327680 | tf_op jit(solution)/shard_map/reduce_scatter | solution.py:79
  71.2 45.6 %copy-start.8 = (bf16[1,64,256]{2,1,0:T(8,128)(2,1)S(1)}, bf16[1,64,256]{2,1,0:T(8,128)(2,1)}, u32[]{:S(2)}) copy-start(bf16[1,64,256]{2,1,0:T(8,128)(2,1)} %param.15) | copy-start | bytes 98308
  85.3 0.7 copy-start.2
  86.0 112.7 %all-reduce.9.cloned.1.call-start = ((), (), s32[]{:S(2)}) async-start(), calls=%async_computation.7 | async-start | bytes 524288 | tf_op jit(solution)/shard_map/psum | solution.py:83
  121.2 6.4 %copy-start.5 = (bf16[64,256]{1,0:T(8,128)(2,1)}, bf16[64,256]{1,0:T(8,128)(2,1)S(1)}, u32[]{:S(2)}) copy-start(bf16[64,256]{1,0:T(8,128)(2,1)S(1)} %fusion.15) | copy-start | bytes 98308
  127.6 11.1 %copy-start.10 = (s32[2,3]{1,0:T(2,128)S(1)}, s32[2,3]{1,0:T(2,128)}, u32[]{:S(2)}) copy-start(s32[2,3]{1,0:T(2,128)} %get-tuple-element.488) | copy-start | bytes 76
  127.6 165.4 %reduce-scatter.6.cloned.1.call-start = ((), (), s32[]{:S(2)}) async-start(), calls=%async_computation.6 | async-start | bytes 278528 | tf_op jit(solution)/shard_map/reduce_scatter | solution.py:104
  138.7 60.0 %copy-start.3 = (f32[256,256]{1,0:T(8,128)S(1)}, f32[256,256]{1,0:T(8,128)}, u32[]{:S(2)}) copy-start(f32[256,256]{1,0:T(8,128)} %all-reduce.7.cloned.1.call-done) | copy-start | bytes 786436
  138.7 154.3 %copy-start.6 = (bf16[1,16,256]{2,1,0:T(8,128)(2,1)S(1)}, bf16[1,16,256]{2,1,0:T(8,128)(2,1)}, u32[]{:S(2)}) copy-start(bf16[1,16,256]{2,1,0:T(8,128)(2,1)} %param.16) | copy-start | bytes 24580
  188.2 0.7 copy-start
  189.0 153.5 %all-reduce.11.cloned.1.call-start = ((), (), s32[]{:S(2)}) async-start(), calls=%async_computation.9 | async-start | bytes 524288 | tf_op jit(solution)/shard_map/psum | solution.py:108
  296.8 20.8 %copy-start.9 = (bf16[16,256]{1,0:T(8,128)(2,1)}, bf16[16,256]{1,0:T(8,128)(2,1)S(1)}, u32[]{:S(2)}) copy-start(bf16[16,256]{1,0:T(8,128)(2,1)S(1)} %fusion.18) | copy-start | bytes 24580
  317.5 122.4 %reduce-scatter.8.cloned.1.call-start = ((), (), s32[]{:S(2)}) async-start(), calls=%async_computation.8 | async-start | bytes 278528 | tf_op jit(solution)/shard_map/reduce_scatter | solution.py:120
  317.6 24.9 %copy-start.4 = (f32[256,256]{1,0:T(8,128)S(1)}, f32[256,256]{1,0:T(8,128)}, u32[]{:S(2)}) copy-start(f32[256,256]{1,0:T(8,128)} %all-reduce.9.cloned.1.call-done) | copy-start | bytes 786436
  317.6 122.3 %copy-start.7 = (bf16[1,16,256]{2,1,0:T(8,128)(2,1)S(1)}, bf16[1,16,256]{2,1,0:T(8,128)(2,1)}, u32[]{:S(2)}) copy-start(bf16[1,16,256]{2,1,0:T(8,128)(2,1)} %param.17) | copy-start | bytes 24580
  341.7 0.7 copy-start.1
Sparse Core Ops, SparseCore 0:
  52.4 14.0 all-reduce.6
  71.2 22.1 all-reduce.4
  127.7 70.9 all-reduce.8
  317.6 20.5 all-reduce.10
Sparse Core Ops, SparseCore 1:
  86.1 30.6 reduce-scatter.3
  189.0 103.9 reduce-scatter.5
  342.5 97.3 reduce-scatter.7
where the time goes:
time: 454 us; the launch traced here: 452 us
  waiting for transfers between devices  202 us (44%)
  blocking collectives  86.3 us (19%)
  matrix products  54.4 us (12%)
  local copies, waits for them, and re-layouts  45.9 us (10%)
  other arithmetic  22.2 us (5%)
  loops' own time  20.3 us (4%)
  between operations  20.1 us (4%)
    reduce_scatter x1, waiting for transfers between devices, on_device(): lax.psum_scatter(partial_c, ('gx', 'gy'), scatter_dimension=0, tiled=True)  87.5 us
    reduce_scatter x1, waiting for transfers between devices, on_device(): lax.psum_scatter(partial_b, ('gx', 'gz'), scatter_dimension=0, tiled=True)  84.3 us
    all_gather x1, blocking collectives, on_device(): slab_c = lax.all_gather(own_c, ('gx', 'gy'), axis=0, tiled=True)  43.3 us
    while x3, local copies, waits for them, and re-layouts  24.6 us
    all_gather x1, blocking collectives, on_device(): slab_b_new = lax.all_gather(new_b, ('gx', 'gz'), axis=0, tiled=True)  19.8 us
    all_gather x1, blocking collectives, on_device(): slab_b = lax.all_gather(own_b, ('gx', 'gz'), axis=0, tiled=True)  17.8 us
    dot_general x1, matrix products, second_visit(): lax.dot_general(band_a, block.reshape(side, side * side), (((0,), (0,)),...  15 us
    reduce_scatter x1, waiting for transfers between devices, on_device(): lax.psum_scatter(partial_a, ('gy', 'gz'), scatter_dimension=0, tiled=True)  13.3 us
  transfers between devices with their start and end apart: 7, of which 5 were waited for; matrix products, arithmetic and copies ran while one was open for 23% of the time, Pallas kernels for 0%

commit v1 on v0

--- a/solution.py
+++ b/solution.py
@@ -6,6 +6,24 @@
 NS_STEPS = 8
 ADMM_ITERS = 4
 HIGHEST = lax.Precision.HIGHEST
+
+
+def in_order(blocks, dim):
+    shape = list(blocks.shape[1:])
+    shape[dim] *= blocks.shape[0]
+    return jnp.moveaxis(blocks, 0, dim).reshape(shape)
+
+
+def grow_blocks(array, axis):
+    length = lax.axis_size(axis)
+    parts = array[None]
+    for level in range(length.bit_length() - 1):
+        distance = 1 << level
+        partner_block = lax.ppermute(parts, axis, [(i, i ^ distance) for i in range(length)])
+        both = jnp.stack([parts, partner_block])
+        upper = lax.axis_index(axis) >> level & 1
+        parts = jnp.where(upper == 0, both, both[::-1]).reshape(-1, *array.shape)
+    return parts
 
 
 def gram_rows(factor):
@@ -50,7 +68,7 @@
     own_b = factor_b[0]
     own_c = factor_c[0]
     slab_b = lax.all_gather(own_b, ("gx", "gz"), axis=0, tiled=True)
-    slab_c = lax.all_gather(own_c, ("gx", "gy"), axis=0, tiled=True)
+    slab_c = in_order(grow_blocks(own_c, ("gx", "gy")), 0)
     height = slab_b.shape[0]
     gram_b = lax.psum(gram_rows(slab_b), "gy")
     gram_c = lax.psum(gram_rows(slab_c), "gz")

time: 454 us -> 433 us (0.954)
  blocking collectives: 86.3 us -> 46.3 us
  waiting for transfers between devices: 202 us -> 214 us
  starting transfers between devices: 0.51 us -> 7.87 us
    all_gather x1 -> x0, blocking collectives: 43.3 us -> none  [on_device(): slab_c = lax.all_gather(own_c, ('gx', 'gy'), axis=0, tiled=True)]
    psum x1, waiting for transfers between devices: 0.02 us -> 20.6 us  [on_device(): gram_c = lax.psum(gram_rows(slab_c), 'gz')]
    reduce_scatter x1, waiting for transfers between devices: 13.3 us -> 0.03 us  [on_device(): lax.psum_scatter(partial_a, ('gy', 'gz'), scatter_dimension=0, tiled=True)]
    ppermute x0 -> x4, waiting for transfers between devices: none -> 7.78 us  [grow_blocks(): lax.ppermute(parts, axis, [(i, i ^ distance) for i in range(length)])]
    ppermute x0 -> x4, starting transfers between devices: none -> 7.36 us  [grow_blocks(): lax.ppermute(parts, axis, [(i, i ^ distance) for i in range(length)])]
  transfers between devices with their start and end apart: 7 -> 11, of which waited for: 5 -> 8; matrix products, arithmetic and copies ran while one was open for 23% -> 25% of each run, Pallas kernels for 0% -> 0%
where the time goes in v1:
time: 433 us; the launch traced here: 432 us
  waiting for transfers between devices  214 us (49%)
  matrix products  54.4 us (13%)
  blocking collectives  46.3 us (11%)
  local copies, waits for them, and re-layouts  45.9 us (11%)
  other arithmetic  23 us (5%)
  loops' own time  20.2 us (5%)
  between operations  20.2 us (5%)
  starting transfers between devices  7.87 us (2%)
    reduce_scatter x1, waiting for transfers between devices, on_device(): lax.psum_scatter(partial_c, ('gx', 'gy'), scatter_dimension=0, tiled=True)  87.5 us
    reduce_scatter x1, waiting for transfers between devices, on_device(): lax.psum_scatter(partial_b, ('gx', 'gz'), scatter_dimension=0, tiled=True)  84.1 us
    while x3, local copies, waits for them, and re-layouts  24.6 us
    all_gather x1, blocking collectives, on_device(): slab_b = lax.all_gather(own_b, ('gx', 'gz'), axis=0, tiled=True)  21.1 us
    psum x1, waiting for transfers between devices, on_device(): gram_c = lax.psum(gram_rows(slab_c), 'gz')  20.6 us
    all_gather x1, blocking collectives, on_device(): slab_b_new = lax.all_gather(new_b, ('gx', 'gz'), axis=0, tiled=True)  19.8 us
    dot_general x1, matrix products, second_visit(): lax.dot_general(band_a, block.reshape(side, side * side), (((0,), (0,)),...  15 us
    dot_general x12, matrix products, split_updates(): jnp.dot(totals + penalty * (primal + dual), inverse, precision=HIGHEST)  12.6 us
  transfers between devices with their start and end apart: 11, of which 8 were waited for; matrix products, arithmetic and copies ran while one was open for 25% of the time, Pallas kernels for 0%

profile of v1, /device:TPU:0, one launch (start us, length us, event | category | flops | bytes accessed | tf_op | source)
XLA Modules:
  0.0 431.6 jit_solution(9585368864245833262)
XLA Ops:
  8.0 3.0 collective-permute-start
  13.6 2.1 collective-permute-start.1
  17.5 2.1 collective-permute-start.2
  19.6 21.1 %all-gather = bf16[1,256,256]{2,1,0:T(8,128)(2,1)S(1)} all-gather(bf16[1,16,256]{2,1,0:T(8,128)(2,1)} %param.16), channel_id=2, replica_groups=mesh['gx'=8,'gy'=2,'gz'=2] {'gx','gz'}, dimensions={1}, use_global_device_ids=true | all-gather | bytes 139264 | tf_op jit(solution)/shard_map/all_gather | solution.py:70
  41.8 4.2 collective-permute-done.3
  47.2 14.0 %while.32 = (s32[]{:T(128)}, f32[256,256]{1,0:T(8,128)S(1)}, s32[]{:T(128)}, s32[2,3]{1,0:T(2,128)}, bf16[2,128,128,128]{3,2,1,0:T(8,128)(2,1)}, /*index=5*/bf16...) while((s32[]{:T(128)}, f32[256,256]{1,0:T(8,128)S(1)}, ...), condition=%wide.region_2.3_spmd, body=%wide.region_0.2_spmd.sunk | while | flops 1082163200 | bytes 5374269 | solution.py:96
  53.0 4.5 %multiply_reduce_fusion.4 = f32[128,256]{1,0:T(8,128)S(1)} fusion(f32[128,256]{1,0:T(8,128)S(1)} %dynamic-slice_convert_fusion.2, bf16[2,128,128,128]{3,2,1,0:T(8,128)(2,1)} %get-tuple-element.401, s32[]{:T(128)S(6)} %select_n.128, bf16[256,256]{1,0:T(8,128)(2,1)S(1)} %get-tuple-element.402, s32[]{:T(128)S(6)} %select_n.130), kind=kOutput, calls=%fused_computation.clone.1 | convolution fusion | flops 1082097664 | bytes 4521992 | tf_op jit(solution)/shard_map/while/body/dot_general | solution.py:89
  61.9 2.9 all-reduce.5.cloned.1.call-done
  64.8 20.6 %all-reduce.7.cloned.1.call-done = f32[256,256]{1,0:T(8,128)} async-done(((f32[256,256]{1,0:T(8,128)}), f32[256,256]{1,0:T(8,128)}) %all-reduce.7.cloned.1.call-update) | async-done | bytes 262160 | tf_op jit(solution)/shard_map/psum | solution.py:74
  100.0 5.4 %all_gather.10 = bf16[256,256]{1,0:T(8,128)(2,1)S(1)} all-gather(bf16[64,256]{1,0:T(8,128)(2,1)S(1)} %fusion.15), channel_id=1, replica_groups=mesh['gx'=8,'gy'=2,'gz'=2] {'gy','gz'}, dimensions={0}, use_global_device_ids=true | all-gather | bytes 163840 | tf_op jit(solution)/shard_map/all_gather | solution.py:100
  106.4 11.0 %broadcast_in_dim.28 = f32[2,256,16384]{2,1,0:T(8,128)} broadcast(f32[]{:T(128)} %constant.96.clone.1), dimensions={} | broadcast | bytes 33554436 | tf_op jit(solution)/shard_map/broadcast_in_dim | solution.py:120
  117.5 49.5 %while.33 = (s32[]{:T(128)}, f32[256,256]{1,0:T(8,128)S(1)}, f32[2,256,16384]{2,1,0:T(8,128)}, s32[]{:T(128)}, s32[2,3]{1,0:T(2,128)S(1)}, /*index=5*/bf16[256,2...) while((s32[]{:T(128)}, f32[256,256]{1,0:T(8,128)S(1)}, ...), condition=%wide.region_11.12_spmd, body=%wide.region_9.11_spmd.sunk | while | flops 1082163200 | bytes 98697544 | solution.py:121
  121.1 2.5 constant_dynamic-slice_fusion.14
  123.6 15.0 %bitcast_dynamic-update-slice_fusion.2 = (f32[2,256,16384]{2,1,0:T(8,128)}, f32[256,16384]{1,0:T(8,128)}) fusion(f32[2,256,16384]{2,1,0:T(8,128)} %get-tuple-element.422, s32[]{:T(128)S(6)} %select_n.132, bf16[16,8,128,128]{3,2,1,0:T(8,128)(2,1)S(1)} %bitcast.205, bf16[256,256]{1,0:T(8,128)(2,1)S(1)} %get-tuple-element.437, s32[]{:T(128)S(6)} %select_n.134), kind=kOutput, calls=%fused_computation.10.clone.1 | convolution fusion | flops 1073741824 | bytes 37814280 | tf_op jit(solution)/shard_map/while/body/dot_general | solution.py:108
  138.6 14.1 %copy.55 = f32[32,8,128,128]{3,2,1,0:T(8,128)} copy(f32[32,8,128,128]{3,1,2,0:T(8,128)} %bitcast.204) | data formatting | bytes 33554432 | tf_op jit(solution)/shard_map/while
  154.8 8.2 %multiply_reduce_fusion.5 = f32[256,128]{1,0:T(8,128)S(1)} fusion(f32[256,128,128]{2,1,0:T(8,128)} %bitcast.203, f32[256,128]{1,0:T(8,128)S(1)} %convert_bitcast_fusion.4), kind=kLoop, calls=%fused_computation.11.clone.1 | loop fusion | flops 8355840 | bytes 17039360 | tf_op jit(solution)/shard_map/while/body/reduce_sum | solution.py:114
  168.0 10.8 %all-reduce.9.cloned.1.call-done = f32[256,256]{1,0:T(8,128)} async-done(((f32[256,256]{1,0:T(8,128)}), f32[256,256]{1,0:T(8,128)}) %all-reduce.9.cloned.1.call-update) | async-done | bytes 262160 | tf_op jit(solution)/shard_map/psum | solution.py:101
  188.8 84.1 %reduce-scatter.6.cloned.1.call-done = f32[16,256]{1,0:T(8,128)} async-done(((f32[256,256]{1,0:T(8,128)}), f32[16,256]{1,0:T(8,128)}) %reduce-scatter.6.cloned.1.call-update) | async-done | bytes 16400 | tf_op jit(solution)/shard_map/reduce_scatter | solution.py:122
  276.7 19.8 %all_gather.11 = bf16[256,256]{1,0:T(8,128)(2,1)S(1)} all-gather(bf16[16,256]{1,0:T(8,128)(2,1)S(1)} %fusion.18), channel_id=1, replica_groups=mesh['gx'=8,'gy'=2,'gz'=2] {'gx','gz'}, dimensions={0}, use_global_device_ids=true | all-gather | bytes 139264 | tf_op jit(solution)/shard_map/all_gather | solution.py:125
  297.6 24.1 %while.34 = (s32[]{:T(128)}, f32[256,256]{1,0:T(8,128)S(1)}, s32[]{:T(128)}, s32[2,3]{1,0:T(2,128)S(1)}, f32[2,256,16384]{2,1,0:T(8,128)}, /*index=5*/bf16[256,2...) while((s32[]{:T(128)}, f32[256,256]{1,0:T(8,128)S(1)}, s32[]{:T(128)}, ...), condition=%wide.region_19.20_spmd, body=%wide.region_17.19_spmd.sunk | while | flops 8421390 | bytes 86049016 | solution.py:137
  301.0 6.6 %dynamic-slice_bitcast_fusion.2 = f32[32,8,128,128]{3,1,2,0:T(8,128)S(1)} fusion(f32[2,256,16384]{2,1,0:T(8,128)} %get-tuple-element.468, s32[]{:T(128)S(6)} %select_n.136), kind=kLoop, calls=%fused_computation.26.clone.1 | loop fusion | bytes 33554436 | tf_op jit(solution)/shard_map/while
  307.7 3.8 copy.59
  311.5 6.1 %fusion.284 = f32[256,128]{1,0:T(8,128)S(1)} fusion(f32[32,8,128,128]{3,2,1,0:T(8,128)S(1)} %copy.59, f32[256,128]{1,0:T(8,128)S(1)} %convert_bitcast_fusion.5), kind=kLoop, calls=%fused_computation.25.clone.1 | loop fusion | flops 8355840 | bytes 17039360 | tf_op jit(solution)/shard_map/while/body/reduce_sum | solution.py:132
  332.4 87.5 %reduce-scatter.8.cloned.1.call-done = f32[16,256]{1,0:T(8,128)} async-done(((f32[256,256]{1,0:T(8,128)}), f32[16,256]{1,0:T(8,128)}) %reduce-scatter.8.cloned.1.call-update) | async-done | bytes 16400 | tf_op jit(solution)/shard_map/reduce_scatter | solution.py:138
  (151 shorter events, 55.6 us)
Async XLA Ops:
  8.0 56.8 %all-reduce.5.cloned.1.call-start = ((), (), s32[]{:S(2)}) async-start(), calls=%async_computation.4 | async-start | bytes 524288 | tf_op jit(solution)/shard_map/psum | solution.py:73
  8.0 4.9 %collective-permute-start = (bf16[1,16,256]{2,1,0:T(8,128)(2,1)}, bf16[1,16,256]{2,1,0:T(8,128)(2,1)S(1)}, u32[]{:S(2)}, u32[]{:S(2)}) collective-permute-start(bf16[1,16,256]{2,1,0:T(8,128)(2,1)} %param.17), channel_id=1, source_target_pairs={{0,2},{2,0},{4,6},{6,4},{8,10},{10,8},{12,14},{14,12},{16,18},{18,... | collective-permute-start | bytes 24584 | tf_op jit(solution)/shard_map/ppermute | solution.py:22
  13.6 3.8 collective-permute-start.1
  17.5 23.2 %collective-permute-start.2 = (bf16[4,16,256]{2,1,0:T(8,128)(2,1)S(1)}, bf16[4,16,256]{2,1,0:T(8,128)(2,1)S(1)}, u32[]{:S(2)}, u32[]{:S(2)}) collective-permute-start(bf16[4,16,256]{2,1,0:T(8,128)(2,1)S(1)} %bitcast.211), channel_id=1, source_target_pairs={{0,8},{2,10},{4,12},{6,14},{8,0},{10,2},{12,4},{14,6},{16,24},{18,... | collective-permute-start | bytes 98312 | tf_op jit(solution)/shard_map/ppermute | solution.py:22
  40.8 5.3 %collective-permute-start.3 = (bf16[8,16,256]{2,1,0:T(8,128)(2,1)S(1)}, bf16[8,16,256]{2,1,0:T(8,128)(2,1)S(1)}, u32[]{:S(2)}, u32[]{:S(2)}) collective-permute-start(bf16[8,16,256]{2,1,0:T(8,128)(2,1)S(1)} %bitcast.209), channel_id=1, source_target_pairs={{0,16},{2,18},{4,20},{6,22},{8,24},{10,26},{12,28},{14,30},{16,0},... | collective-permute-start | bytes 196616 | tf_op jit(solution)/shard_map/ppermute | solution.py:22
  41.8 43.6 %all-reduce.7.cloned.1.call-start = ((), (), s32[]{:S(2)}) async-start(), calls=%async_computation.5 | async-start | bytes 524288 | tf_op jit(solution)/shard_map/psum | solution.py:74
  47.1 48.4 %reduce-scatter.4.cloned.1.call-start = ((), (), s32[]{:S(2)}) async-start(), calls=%async_computation.3 | async-start | bytes 327680 | tf_op jit(solution)/shard_map/reduce_scatter | solution.py:97
  47.1 48.4 %copy-start.8 = (bf16[1,64,256]{2,1,0:T(8,128)(2,1)S(1)}, bf16[1,64,256]{2,1,0:T(8,128)(2,1)}, u32[]{:S(2)}) copy-start(bf16[1,64,256]{2,1,0:T(8,128)(2,1)} %param.15) | copy-start | bytes 98308
  61.1 0.7 copy-start.2
  61.9 116.9 %all-reduce.9.cloned.1.call-start = ((), (), s32[]{:S(2)}) async-start(), calls=%async_computation.7 | async-start | bytes 524288 | tf_op jit(solution)/shard_map/psum | solution.py:101
  99.9 6.5 %copy-start.5 = (bf16[64,256]{1,0:T(8,128)(2,1)}, bf16[64,256]{1,0:T(8,128)(2,1)S(1)}, u32[]{:S(2)}) copy-start(bf16[64,256]{1,0:T(8,128)(2,1)S(1)} %fusion.15) | copy-start | bytes 98308
  106.3 11.1 %copy-start.10 = (s32[2,3]{1,0:T(2,128)S(1)}, s32[2,3]{1,0:T(2,128)}, u32[]{:S(2)}) copy-start(s32[2,3]{1,0:T(2,128)} %get-tuple-element.512) | copy-start | bytes 76
  106.3 166.6 %reduce-scatter.6.cloned.1.call-start = ((), (), s32[]{:S(2)}) async-start(), calls=%async_computation.6 | async-start | bytes 278528 | tf_op jit(solution)/shard_map/reduce_scatter | solution.py:122
  117.4 61.3 %copy-start.4 = (f32[256,256]{1,0:T(8,128)S(1)}, f32[256,256]{1,0:T(8,128)}, u32[]{:S(2)}) copy-start(f32[256,256]{1,0:T(8,128)} %all-reduce.7.cloned.1.call-done) | copy-start | bytes 786436
  117.4 155.5 %copy-start.6 = (bf16[1,16,256]{2,1,0:T(8,128)(2,1)S(1)}, bf16[1,16,256]{2,1,0:T(8,128)(2,1)}, u32[]{:S(2)}) copy-start(bf16[1,16,256]{2,1,0:T(8,128)(2,1)} %param.16) | copy-start | bytes 24580
  167.0 0.7 copy-start
  167.7 154.7 %all-reduce.11.cloned.1.call-start = ((), (), s32[]{:S(2)}) async-start(), calls=%async_computation.9 | async-start | bytes 524288 | tf_op jit(solution)/shard_map/psum | solution.py:126
  276.7 20.8 %copy-start.9 = (bf16[16,256]{1,0:T(8,128)(2,1)}, bf16[16,256]{1,0:T(8,128)(2,1)S(1)}, u32[]{:S(2)}) copy-start(bf16[16,256]{1,0:T(8,128)(2,1)S(1)} %fusion.18) | copy-start | bytes 24580
  297.5 122.4 %reduce-scatter.8.cloned.1.call-start = ((), (), s32[]{:S(2)}) async-start(), calls=%async_computation.8 | async-start | bytes 278528 | tf_op jit(solution)/shard_map/reduce_scatter | solution.py:138
  297.5 24.9 %copy-start.3 = (f32[256,256]{1,0:T(8,128)S(1)}, f32[256,256]{1,0:T(8,128)}, u32[]{:S(2)}) copy-start(f32[256,256]{1,0:T(8,128)} %all-reduce.9.cloned.1.call-done) | copy-start | bytes 786436
  297.5 122.3 %copy-start.7 = (bf16[1,16,256]{2,1,0:T(8,128)(2,1)S(1)}, bf16[1,16,256]{2,1,0:T(8,128)(2,1)}, u32[]{:S(2)}) copy-start(bf16[1,16,256]{2,1,0:T(8,128)(2,1)} %param.17) | copy-start | bytes 24580
  321.7 0.7 copy-start.1
Sparse Core Ops, SparseCore 0:
  41.9 22.8 all-reduce.4
  67.1 18.2 all-reduce.6
  106.5 72.2 all-reduce.8
  297.6 20.5 all-reduce.10
Sparse Core Ops, SparseCore 1:
  62.0 30.1 reduce-scatter.3
  167.8 105.0 reduce-scatter.5
  322.5 97.3 reduce-scatter.7
